TPU v7x, 32 devices: a whole 2x2x4 slice. The times are simulated.
32 devices in a mesh: chan: 8 (over z, y), seg: 4 (over x, core).
Axes of the slice: x: 2, y: 2, z: 4, core: 2. Of those that a mesh axis runs over, the one named last changes fastest.
Arguments:
- traces: bfloat16 [1024, 8192], P('chan', 'seg'), may hold values from -36 to 36
- pair_bins: int32 [2, 1024, 128], P(None, 'chan'), may hold values from 0 to 255
Outputs:
- correlograms: float32 [65, 256], P(None, 'chan')
All inputs are finite; a program needn't handle non-finite values.
Results may differ from a plain program's by a relative error of at most 0.0029.
Values may be sent and summed in bfloat16 or wider, within the bound.
A program may use at most 64 MiB of HBM per device.

v0:
```python
import functools
import math

import jax
import jax.numpy as jnp
from jax import lax
from jax.experimental import pallas as pl
from jax.experimental.pallas import tpu as pltpu
from jax.sharding import PartitionSpec as P

MAX_LAG = 32
NB = 256
ROUNDS = 2
LAGS = 2 * MAX_LAG + 1
EPSILON = 1e-06

FINE = 8
COARSE = MAX_LAG // FINE
LANES = 128
CHUNKS = 4
MESH = pl.DeviceIdType.MESH
CONTRACT = (((1,), (1,)), ((), ()))


def from_behind(block, axis, distance):
    devices = range(lax.axis_size(axis))
    route = [((i - distance) % len(devices), i) for i in devices]
    return lax.ppermute(block, axis, route)


def coarse_shifts(block):
    length = block.shape[1]
    padded = jnp.pad(block, ((0, 0), (MAX_LAG, MAX_LAG)))
    starts = range(FINE, 2 * MAX_LAG + 1, FINE)
    return jnp.concatenate([lax.slice_in_dim(padded, start, start + length, axis=1) for start in starts], 0)


def stack_kernel(group, first, far_ref, near_ref, scale_ref, bins_ref, prior_ref, out_ref, fine, neg, pos, last):
    channels, length = far_ref.shape
    width = near_ref.shape[0] // (2 * COARSE)

    def dot(left, right):
        return lax.dot_general(left, right, CONTRACT, preferred_element_type=jnp.float32)

    pair = 2
    tile = pair * FINE
    blank = jnp.zeros((FINE, LANES), jnp.float32)
    for block in range(channels // tile):
        wide = far_ref[block * tile : (block + 1) * tile, :].astype(jnp.float32)
        for start in range(0, tile, pair):
            both = []
            for x in range(start, start + pair):
                row = jnp.broadcast_to(wide[x : x + 1], (FINE, length))
                both.append(jnp.concatenate([row, blank], 1))
            rows = slice((block * tile + start) * FINE, (block * tile + start + pair) * FINE)
            for side, base in ((0, LANES + length - FINE), (1, 0)):
                turned = [pltpu.roll(row, base, 1, stride=1, stride_axis=0)[:, :length] for row in both]
                fine[side, rows, :] = jnp.concatenate(turned, 0).astype(jnp.bfloat16)

    neg[...] = dot(fine[0], near_ref[: COARSE * width])
    pos[...] = dot(fine[1], near_ref[(COARSE - 1) * width : (2 * COARSE - 1) * width])
    last[...] = dot(far_ref[...], near_ref[(2 * COARSE - 1) * width :])

    bin_ids = lax.broadcasted_iota(jnp.int32, (NB, width), 0)
    out_ref[...] = jnp.zeros_like(out_ref) if first else prior_ref[...]

    @pl.loop(0, channels // group)
    def _(g):
        base = pl.multiple_of(g * group, group)
        scale = scale_ref[pl.ds(base, group), :]
        bins = bins_ref[pl.ds(base, group), :]
        top = last[pl.ds(base, group), :]
        for half in range(0, group, group // 2):
            scores, hots = [], []
            for x in range(half, half + group // 2):
                rows = pl.ds(pl.multiple_of((base + x) * FINE, FINE), FINE)
                factor = jnp.broadcast_to(scale[x : x + 1], (FINE, width))
                pieces = []
                for side in (neg, pos):
                    for k in range(COARSE):
                        pieces.append(side[rows, k * width : (k + 1) * width] * factor)
                edge = jnp.broadcast_to(top[x : x + 1], (FINE, width)) * factor
                pieces += [edge, edge]
                scores.append(jnp.concatenate(pieces, 0).astype(jnp.bfloat16))
                hit = jnp.broadcast_to(bins[x : x + 1], (NB, width)) == bin_ids
                hots.append(jnp.where(hit, 1.0, 0.0).astype(jnp.bfloat16))
            out_ref[...] += dot(jnp.concatenate(scores, 1), jnp.concatenate(hots, 1))


def chunk_stack(far, near, scale, bins, prior):
    channels, length = far.shape
    width = near.shape[0] // (2 * COARSE)
    lag_rows = 2 * MAX_LAG + 2 * FINE
    first = prior is None
    if first:
        prior = jnp.zeros((8, LANES), jnp.float32)
    return pl.pallas_call(
        functools.partial(stack_kernel, 8, first),
        out_shape=jax.ShapeDtypeStruct((lag_rows, NB), jnp.float32),
        in_specs=[pl.BlockSpec(memory_space=pltpu.VMEM)] * 5,
        out_specs=pl.BlockSpec(memory_space=pltpu.VMEM),
        scratch_shapes=[
            pltpu.VMEM((2, channels * FINE, length), jnp.bfloat16),
            pltpu.VMEM((channels * FINE, COARSE * width), jnp.float32),
            pltpu.VMEM((channels * FINE, COARSE * width), jnp.float32),
            pltpu.VMEM((channels, width), jnp.float32),
        ],
        compiler_params=pltpu.CompilerParams(vmem_limit_bytes=32 * 1024 * 1024),
        cost_estimate=pl.CostEstimate(
            flops=2 * LAGS * channels * width * length, bytes_accessed=near.size * 2, transcendentals=0
        ),
    )(far, near, scale, bins, prior)


def reduce_kernel(n_chan, n_seg, part_ref, out_ref, arrived, mine, others, send1, recv1, send2, recv2):
    chan, seg = lax.axis_index("chan"), lax.axis_index("seg")
    rows = out_ref.shape[0]
    chan_peers = [lax.rem(chan + k, n_chan) for k in range(1, n_chan)]
    seg_peers = [lax.rem(seg + k, n_seg) for k in range(1, n_seg)]
    barrier = pltpu.get_barrier_semaphore()
    for peer in chan_peers:
        pl.semaphore_signal(barrier, inc=1, device_id=(peer, seg), device_id_type=MESH)
    for peer in seg_peers:
        pl.semaphore_signal(barrier, inc=1, device_id=(chan, peer), device_id_type=MESH)
    pl.semaphore_wait(barrier, n_chan + n_seg - 2)

    first = []
    for k, peer in enumerate(chan_peers):
        copy = pltpu.make_async_remote_copy(
            src_ref=part_ref.at[pl.ds(pl.multiple_of(peer * rows, rows), rows)],
            dst_ref=arrived.at[k],
            send_sem=send1.at[k],
            recv_sem=recv1.at[k],
            device_id=(peer, seg),
            device_id_type=MESH,
        )
        copy.start()
        first.append(copy)
    running = part_ref[pl.ds(pl.multiple_of(chan * rows, rows), rows), :]
    for k, copy in enumerate(first):
        copy.wait()
        running = running + arrived[k]
    mine[...] = running
    second = []
    for k, peer in enumerate(seg_peers):
        copy = pltpu.make_async_remote_copy(
            src_ref=mine,
            dst_ref=others.at[k],
            send_sem=send2.at[k],
            recv_sem=recv2.at[k],
            device_id=(chan, peer),
            device_id_type=MESH,
        )
        copy.start()
        second.append(copy)
    for copy in second:
        copy.wait()
    for position in range(n_seg):
        slot = lax.rem(seg - position + n_seg - 1 + n_seg, n_seg)
        term = jnp.where(slot == n_seg - 1, running, others[jnp.minimum(slot, n_seg - 2)])
        sums = term if position == 0 else sums + term
    out_ref[...] = sums


def reduce_all(part):
    n_chan, n_seg = lax.axis_size("chan"), lax.axis_size("seg")
    rows = part.shape[0] // n_chan
    block = (rows, part.shape[1])
    return pl.pallas_call(
        functools.partial(reduce_kernel, n_chan, n_seg),
        out_shape=jax.ShapeDtypeStruct(block, jnp.float32),
        in_specs=[pl.BlockSpec(memory_space=pltpu.VMEM)],
        out_specs=pl.BlockSpec(memory_space=pltpu.VMEM),
        scratch_shapes=[
            pltpu.VMEM((n_chan - 1,) + block, jnp.float32),
            pltpu.VMEM(block, jnp.float32),
            pltpu.VMEM((n_seg - 1,) + block, jnp.float32),
            pltpu.SemaphoreType.DMA((n_chan - 1,)),
            pltpu.SemaphoreType.DMA((n_chan - 1,)),
            pltpu.SemaphoreType.DMA((n_seg - 1,)),
            pltpu.SemaphoreType.DMA((n_seg - 1,)),
        ],
        compiler_params=pltpu.CompilerParams(
            collective_id=0, has_side_effects=True, vmem_limit_bytes=16 * 1024 * 1024
        ),
    )(part)


def local(traces, pair_bins):
    channels, seg_length = traces.shape
    chan_count = lax.axis_size("chan")
    seg_count = lax.axis_size("seg")
    total_time = seg_length * seg_count
    time_scale = 1.0 / math.sqrt(total_time)
    half_loop = chan_count // 2
    next_block = from_behind(traces, "chan", -1)
    next_bins = from_behind(pair_bins[1], "chan", -1)
    size = channels // CHUNKS
    far_chunks = [from_behind(traces[k * size : (k + 1) * size], "chan", -half_loop) for k in range(CHUNKS)]
    energy = lax.psum(jnp.sum(jnp.square(traces.astype(jnp.float32)), axis=1), "seg")
    scale = lax.rsqrt(energy / total_time + EPSILON)
    far_scale = from_behind(scale, "chan", -half_loop)
    next_scale = from_behind(scale, "chan", -1)
    near = coarse_shifts(jnp.concatenate([traces, next_block], 0))
    near_scale = jnp.concatenate([scale, next_scale], 0)
    pair_scale = far_scale[:, None] * near_scale[None, :] * time_scale
    bins = jnp.concatenate([pair_bins[0], next_bins], 0).T
    part = None
    for k, chunk in enumerate(far_chunks):
        rows = slice(k * size, (k + 1) * size)
        part = chunk_stack(chunk, near, pair_scale[rows], bins[rows], part)
    pair_total = ROUNDS * chan_count * channels * channels // NB
    part = part.T * (1.0 / math.sqrt(pair_total))
    part = jnp.pad(part, ((0, 0), (0, -part.shape[1] % LANES)))
    return reduce_all(part).T[:LAGS][::-1]


def solution(mesh):
    in_specs = (P("chan", "seg"), P(None, "chan", None))
    out_specs = P(None, "chan")
    return jax.shard_map(local, mesh=mesh, in_specs=in_specs, out_specs=out_specs, check_vma=False)
```

profile of v0, /device:TPU:0, one launch (start us, length us, event | category | flops | bytes accessed | tf_op | source)
XLA Modules:
  0.0 64.1 jit_solution(1004223083836098320)
XLA Ops:
  0.0 6.0 %collective-permute-start.1 = (bf16[128,2048]{1,0:T(8,128)(2,1)}, bf16[128,2048]{1,0:T(8,128)(2,1)S(1)}, u32[]{:S(2)}, u32[]{:S(2)}) collective-permute-start(bf16[128,2048]{1,0:T(8,128)(2,1)} %param.2), channel_id=1, source_target_pairs={{4,0},{8,4},{12,8},{16,12},{20,16},{24,20},{28,24},{0,28},{5,1},{9... | collective-permute-start | bytes 1572872 | tf_op jit(solution)/shard_map/ppermute | solution.py:28
  6.0 1.3 %multiply_reduce_fusion = f32[128]{0:T(128)S(1)} fusion(bf16[128,2048]{1,0:T(8,128)(2,1)} %param.2), kind=kLoop, calls=%fused_computation.13 | loop fusion | flops 786304 | bytes 524800 | tf_op jit(solution)/shard_map/reduce_sum | solution.py:200
  7.3 6.6 %psum.7 = f32[128]{0:T(128)S(1)} all-reduce(f32[128]{0:T(128)S(1)} %multiply_reduce_fusion), channel_id=1, replica_groups=mesh['chan'=8,'seg'=4] {'seg'}, use_global_device_ids=true, to_apply=%region_1.0 | all-reduce | flops 128 | bytes 1024 | tf_op jit(solution)/shard_map/psum | solution.py:200
  14.2 0.9 %fusion.7 = (s32[1,128,128]{2,1,0:T(8,128)S(1)}, s32[1,128,128]{2,1,0:T(8,128)S(1)}) fusion(s32[2,128,128]{2,1,0:T(8,128)} %param.3), kind=kLoop, calls=%fused_computation.24 | loop fusion | bytes 262144 | tf_op jit(solution)/shard_map/slice | solution.py:207
  15.1 2.1 %collective-permute-start.4 = (s32[128,128]{0,1:T(8,128)S(1)}, s32[128,128]{0,1:T(8,128)S(1)}, u32[]{:S(2)}, u32[]{:S(2)}) collective-permute-start(s32[128,128]{0,1:T(8,128)S(1)} %bitcast.10), channel_id=1, source_target_pairs={{4,0},{8,4},{12,8},{16,12},{20,16},{24,20},{28,24},{0,28},{5,1},{9... | collective-permute-start | bytes 196616 | tf_op jit(solution)/shard_map/ppermute | solution.py:28
  17.2 1.1 %fusion.4 = (bf16[32,2048]{1,0:T(8,128)(2,1)S(1)}, bf16[32,2048]{1,0:T(8,128)(2,1)S(1)}, bf16[32,2048]{1,0:T(8,128)(2,1)S(1)}, bf16[32,2048]{1,0:T(8,128)(2,1)S(1)}) fusion(bf16[128,2048]{1,0:T(8,128)(2,1)} %param.2), kind=kLoop, calls=%fused_computation.21 | loop fusion | bytes 1048576 | tf_op jit(solution)/shard_map/slice | solution.py:199
  18.3 1.8 %collective-permute-start.7 = (bf16[32,2048]{1,0:T(8,128)(2,1)S(1)}, bf16[32,2048]{1,0:T(8,128)(2,1)S(1)}, u32[]{:S(2)}, u32[]{:S(2)}) collective-permute-start(bf16[32,2048]{1,0:T(8,128)(2,1)S(1)} %get-tuple-element.5), channel_id=1, source_target_pairs={{16,0},{20,4},{24,8},{28,12},{0,16},{4,20},{8,24},{12,28},{17,1},{... | collective-permute-start | bytes 393224 | tf_op jit(solution)/shard_map/ppermute | solution.py:28
  20.2 1.3 %collective-permute-start.6 = (bf16[32,2048]{1,0:T(8,128)(2,1)S(1)}, bf16[32,2048]{1,0:T(8,128)(2,1)S(1)}, u32[]{:S(2)}, u32[]{:S(2)}) collective-permute-start(bf16[32,2048]{1,0:T(8,128)(2,1)S(1)} %get-tuple-element.8), channel_id=1, source_target_pairs={{16,0},{20,4},{24,8},{28,12},{0,16},{4,20},{8,24},{12,28},{17,1},{... | collective-permute-start | bytes 393224 | tf_op jit(solution)/shard_map/ppermute | solution.py:28
  21.5 1.8 %collective-permute-start.5 = (bf16[32,2048]{1,0:T(8,128)(2,1)S(1)}, bf16[32,2048]{1,0:T(8,128)(2,1)S(1)}, u32[]{:S(2)}, u32[]{:S(2)}) collective-permute-start(bf16[32,2048]{1,0:T(8,128)(2,1)S(1)} %get-tuple-element.6), channel_id=1, source_target_pairs={{16,0},{20,4},{24,8},{28,12},{0,16},{4,20},{8,24},{12,28},{17,1},{... | collective-permute-start | bytes 393224 | tf_op jit(solution)/shard_map/ppermute | solution.py:28
  23.4 1.3 %collective-permute-start = (bf16[32,2048]{1,0:T(8,128)(2,1)S(1)}, bf16[32,2048]{1,0:T(8,128)(2,1)S(1)}, u32[]{:S(2)}, u32[]{:S(2)}) collective-permute-start(bf16[32,2048]{1,0:T(8,128)(2,1)S(1)} %get-tuple-element.7), channel_id=1, source_target_pairs={{16,0},{20,4},{24,8},{28,12},{0,16},{4,20},{8,24},{12,28},{17,1},{... | collective-permute-start | bytes 393224 | tf_op jit(solution)/shard_map/ppermute | solution.py:28
  24.7 1.5 %fusion.3 = bf16[256,2112]{1,0:T(8,128)(2,1)S(1)} fusion(bf16[128,2048]{1,0:T(8,128)(2,1)S(1)} %collective-permute-done.1, bf16[128,2048]{1,0:T(8,128)(2,1)} %param.2), kind=kLoop, calls=%fused_computation.5 | loop fusion | flops 4866048 | bytes 2129920 | tf_op jit(solution)/shard_map/concatenate | solution.py:204
  26.2 0.4 slice_dynamic-update-slice_fusion.6
  26.6 0.4 slice_dynamic-update-slice_fusion.5
  27.0 0.4 slice_dynamic-update-slice_fusion.4
  27.6 0.4 slice_dynamic-update-slice_fusion.3
  28.0 0.4 slice_dynamic-update-slice_fusion.2
  28.4 0.4 slice_dynamic-update-slice_fusion.1
  29.2 6.7 %collective-permute-done.7.far_ref = bf16[32,2048]{1,0:T(8,128)(2,1)S(1)} collective-permute-done((bf16[32,2048]{1,0:T(8,128)(2,1)S(1)}, bf16[32,2048]{1,0:T(8,128)(2,1)S(1)}, u32[]{:S(2)}, u32[]{:S(2)}) %collective-permute-start.7) | collective-permute-done | bytes 131104 | tf_op jit(solution)/shard_map/ppermute | solution.py:28
  35.9 4.6 %shard_map.28.prior_ref = f32[80,256]{1,0:T(8,128)S(1)} custom-call(bf16[32,2048]{1,0:T(8,128)(2,1)S(1)} %collective-permute-done.7.far_ref, bf16[2048,2048]{1,0:T(8,128)(2,1)S(1)} %slice_dynamic-update-slice_fusion.near_ref, f32[32,256]{1,0:T(8,128)S(1)} %get-tuple-element.13.scale_ref, s32[32,256]{1,0:T(8,128)S(1)} %get-tuple-element.9.bins_ref, ...), custom_call_target="tpu_custom_call" | custom-call | flops 2181038080 | bytes 8388608 | tf_op jit(solution)/shard_map/pallas_call | solution.py:97
  40.5 4.5 %shard_map.29.prior_ref = f32[80,256]{1,0:T(8,128)S(1)} custom-call(bf16[32,2048]{1,0:T(8,128)(2,1)S(1)} %collective-permute-done.6.far_ref, bf16[2048,2048]{1,0:T(8,128)(2,1)S(1)} %slice_dynamic-update-slice_fusion.near_ref, f32[32,256]{1,0:T(8,128)S(1)} %get-tuple-element.14.scale_ref, s32[32,256]{1,0:T(8,128)S(1)} %get-tuple-element.10.bins_ref, ...), custom_call_target="tpu_custom_call" | custom-call | flops 2181038080 | bytes 8388608 | tf_op jit(solution)/shard_map/pallas_call | solution.py:97
  45.0 4.5 %shard_map.30.prior_ref = f32[80,256]{1,0:T(8,128)S(1)} custom-call(bf16[32,2048]{1,0:T(8,128)(2,1)S(1)} %collective-permute-done.5.far_ref, bf16[2048,2048]{1,0:T(8,128)(2,1)S(1)} %slice_dynamic-update-slice_fusion.near_ref, f32[32,256]{1,0:T(8,128)S(1)} %get-tuple-element.15.scale_ref, s32[32,256]{1,0:T(8,128)S(1)} %get-tuple-element.11.bins_ref, ...), custom_call_target="tpu_custom_call" | custom-call | flops 2181038080 | bytes 8388608 | tf_op jit(solution)/shard_map/pallas_call | solution.py:97
  49.5 4.5 %shard_map.31 = f32[80,256]{1,0:T(8,128)S(1)} custom-call(bf16[32,2048]{1,0:T(8,128)(2,1)S(1)} %collective-permute-done.far_ref, bf16[2048,2048]{1,0:T(8,128)(2,1)S(1)} %slice_dynamic-update-slice_fusion.near_ref, f32[32,256]{1,0:T(8,128)S(1)} %get-tuple-element.16.scale_ref, s32[32,256]{1,0:T(8,128)S(1)} %get-tuple-element.12.bins_ref, ...), custom_call_target="tpu_custom_call" | custom-call | flops 2181038080 | bytes 8388608 | tf_op jit(solution)/shard_map/pallas_call | solution.py:97
  54.1 9.3 %shard_map.32 = f32[32,128]{1,0:T(8,128)S(1)} custom-call(f32[256,128]{1,0:T(8,128)S(1)} %pad.9.part_ref), custom_call_target="tpu_custom_call" | custom-call | tf_op jit(solution)/shard_map/pallas_call | solution.py:169
  63.4 0.7 %rev.3 = f32[65,32]{0,1:T(8,128)} reverse(f32[65,32]{0,1:T(8,128)S(1)} %bitcast.8), dimensions={0} | reverse | bytes 16640 | tf_op jit(solution)/shard_map/rev | solution.py:215
  (26 shorter events, 1.2 us)
Async XLA Ops:
  0.0 27.5 %copy-start = (bf16[128,2048]{1,0:T(8,128)(2,1)S(1)}, bf16[128,2048]{1,0:T(8,128)(2,1)}, u32[]{:S(2)}) copy-start(bf16[128,2048]{1,0:T(8,128)(2,1)} %param.2) | copy-start | bytes 1572868
  0.0 24.7 %collective-permute-start.1 = (bf16[128,2048]{1,0:T(8,128)(2,1)}, bf16[128,2048]{1,0:T(8,128)(2,1)S(1)}, u32[]{:S(2)}, u32[]{:S(2)}) collective-permute-start(bf16[128,2048]{1,0:T(8,128)(2,1)} %param.2), channel_id=1, source_target_pairs={{4,0},{8,4},{12,8},{16,12},{20,16},{24,20},{28,24},{0,28},{5,1},{9... | collective-permute-start | bytes 1572872 | tf_op jit(solution)/shard_map/ppermute | solution.py:28
  13.9 6.3 %collective-permute-start.3 = (f32[128]{0:T(128)S(1)}, f32[128]{0:T(128)S(1)}, u32[]{:S(2)}, u32[]{:S(2)}) collective-permute-start(f32[128]{0:T(128)S(1)} %add_rsqrt_fusion), channel_id=1, source_target_pairs={{4,0},{8,4},{12,8},{16,12},{20,16},{24,20},{28,24},{0,28},{5,1},{9... | collective-permute-start | bytes 1544 | tf_op jit(solution)/shard_map/ppermute | solution.py:28
  14.1 7.4 %collective-permute-start.2 = (f32[128]{0:T(128)S(1)}, f32[128]{0:T(128)S(1)}, u32[]{:S(2)}, u32[]{:S(2)}) collective-permute-start(f32[128]{0:T(128)S(1)} %add_rsqrt_fusion), channel_id=1, source_target_pairs={{16,0},{20,4},{24,8},{28,12},{0,16},{4,20},{8,24},{12,28},{17,1},{... | collective-permute-start | bytes 1544 | tf_op jit(solution)/shard_map/ppermute | solution.py:28
  15.1 8.3 %collective-permute-start.4 = (s32[128,128]{0,1:T(8,128)S(1)}, s32[128,128]{0,1:T(8,128)S(1)}, u32[]{:S(2)}, u32[]{:S(2)}) collective-permute-start(s32[128,128]{0,1:T(8,128)S(1)} %bitcast.10), channel_id=1, source_target_pairs={{4,0},{8,4},{12,8},{16,12},{20,16},{24,20},{28,24},{0,28},{5,1},{9... | collective-permute-start | bytes 196616 | tf_op jit(solution)/shard_map/ppermute | solution.py:28
  18.3 17.5 %collective-permute-start.7 = (bf16[32,2048]{1,0:T(8,128)(2,1)S(1)}, bf16[32,2048]{1,0:T(8,128)(2,1)S(1)}, u32[]{:S(2)}, u32[]{:S(2)}) collective-permute-start(bf16[32,2048]{1,0:T(8,128)(2,1)S(1)} %get-tuple-element.5), channel_id=1, source_target_pairs={{16,0},{20,4},{24,8},{28,12},{0,16},{4,20},{8,24},{12,28},{17,1},{... | collective-permute-start | bytes 393224 | tf_op jit(solution)/shard_map/ppermute | solution.py:28
  20.2 20.3 %collective-permute-start.6 = (bf16[32,2048]{1,0:T(8,128)(2,1)S(1)}, bf16[32,2048]{1,0:T(8,128)(2,1)S(1)}, u32[]{:S(2)}, u32[]{:S(2)}) collective-permute-start(bf16[32,2048]{1,0:T(8,128)(2,1)S(1)} %get-tuple-element.8), channel_id=1, source_target_pairs={{16,0},{20,4},{24,8},{28,12},{0,16},{4,20},{8,24},{12,28},{17,1},{... | collective-permute-start | bytes 393224 | tf_op jit(solution)/shard_map/ppermute | solution.py:28
  21.5 23.5 %collective-permute-start.5 = (bf16[32,2048]{1,0:T(8,128)(2,1)S(1)}, bf16[32,2048]{1,0:T(8,128)(2,1)S(1)}, u32[]{:S(2)}, u32[]{:S(2)}) collective-permute-start(bf16[32,2048]{1,0:T(8,128)(2,1)S(1)} %get-tuple-element.6), channel_id=1, source_target_pairs={{16,0},{20,4},{24,8},{28,12},{0,16},{4,20},{8,24},{12,28},{17,1},{... | collective-permute-start | bytes 393224 | tf_op jit(solution)/shard_map/ppermute | solution.py:28
  23.4 26.1 %collective-permute-start = (bf16[32,2048]{1,0:T(8,128)(2,1)S(1)}, bf16[32,2048]{1,0:T(8,128)(2,1)S(1)}, u32[]{:S(2)}, u32[]{:S(2)}) collective-permute-start(bf16[32,2048]{1,0:T(8,128)(2,1)S(1)} %get-tuple-element.7), channel_id=1, source_target_pairs={{16,0},{20,4},{24,8},{28,12},{0,16},{4,20},{8,24},{12,28},{17,1},{... | collective-permute-start | bytes 393224 | tf_op jit(solution)/shard_map/ppermute | solution.py:28
where the time goes:
time: 64.4 us; the launch traced here: 64.1 us
  Pallas kernels  27.3 us (42%)
  starting transfers between devices  14.5 us (23%)
  waiting for transfers between devices  6.73 us (10%)
  blocking collectives  6.59 us (10%)
  local copies, waits for them, and re-layouts  5.88 us (9%)
  other arithmetic  2.85 us (4%)
    pallas_call x4, Pallas kernels, chunk_stack(): pl.pallas_call(functools.partial(stack_kernel, 8, first), out_shape=jax.S...  18 us
    ppermute x8, starting transfers between devices, from_behind(): return lax.ppermute(block, axis, route)  14.5 us
    pallas_call x1, Pallas kernels, reduce_all(): pl.pallas_call(functools.partial(reduce_kernel, n_chan, n_seg), out_shape...  9.28 us
    ppermute x8, waiting for transfers between devices, from_behind(): return lax.ppermute(block, axis, route)  6.73 us
    psum x1, blocking collectives, local(): lax.psum(jnp.sum(jnp.square(traces.astype(jnp.float32)), axis=1), 'seg')  6.59 us
    unnamed x12, local copies, waits for them, and re-layouts  2.67 us
    concatenate x1, other arithmetic, local(): near = coarse_shifts(jnp.concatenate([traces, next_block], 0))  1.47 us
  transfers between devices with their start and end apart: 8, of which 1 were waited for; matrix products, arithmetic and copies ran while one was open for 12% of the time, Pallas kernels for 21%

commit v1 on v0

v1 whole, which is shorter than its diff:
```python
import functools
import math

import jax
import jax.numpy as jnp
from jax import lax
from jax.experimental import pallas as pl
from jax.experimental.pallas import tpu as pltpu
from jax.sharding import PartitionSpec as P

MAX_LAG = 32
NB = 256
ROUNDS = 2
LAGS = 2 * MAX_LAG + 1
EPSILON = 1e-06

FINE = 8
COARSE = 2 * MAX_LAG // FINE
LANES = 128
ROWS = 80
MESH = pl.DeviceIdType.MESH
CONTRACT = (((1,), (1,)), ((), ()))
F32, BF16 = jnp.float32, jnp.bfloat16


def dot(left, right):
    return lax.dot_general(left, right, CONTRACT, preferred_element_type=F32)


def lane_mask(rows, low, high):
    lane = lax.broadcasted_iota(jnp.int32, (rows, LANES), 1)
    return jnp.where((lane >= low) & (lane < high), 1.0, 0.0).astype(BF16)


def near_shifts(source, shifted):
    rows, length = source.shape
    block = source[...]
    for k in range(COARSE):
        step = FINE * (k - COARSE // 2)
        at = slice(k * rows, (k + 1) * rows)
        if step == 0:
            shifted[at, :] = block
            continue
        turned = pltpu.roll(block, step % length, 1)
        if step > 0:
            shifted[at, :LANES] = turned[:, :LANES] * lane_mask(rows, step, LANES)
            shifted[at, LANES:] = turned[:, LANES:]
        else:
            keep = 1 - lane_mask(rows, LANES + step, LANES - FINE)
            shifted[at, : length - LANES] = turned[:, : length - LANES]
            shifted[at, length - LANES :] = turned[:, length - LANES :] * keep


def centre_shifts(block, fine):
    rows, length = block.shape
    for f in range(FINE + 1):
        at = slice(f * rows, (f + 1) * rows)
        if f == 0:
            fine[at, :length] = block
            fine[at, length:] = block[:, length - LANES :] * lane_mask(rows, 0, LANES - FINE)
            continue
        turned = pltpu.roll(block, length - f, 1)
        tail = turned[:, length - LANES :]
        fine[at, : length - LANES] = turned[:, : length - LANES]
        fine[at, length - LANES : length] = tail * lane_mask(rows, 0, LANES - f)
        if f < FINE:
            fine[at, length:] = tail * (1 - lane_mask(rows, LANES - FINE, LANES - f))


def correlate(fine, near, raw):
    width = near.shape[0] // COARSE
    length = near.shape[1]
    total = fine.shape[0]
    rows = total // (FINE + 1)
    plain = FINE * rows
    wrapped = jnp.concatenate([fine[:plain, : length - LANES], fine[:plain, length:]], 1)
    half = COARSE // 2
    spans = ((0, half, wrapped), (half, COARSE - 2, fine[:plain, :length]), (COARSE - 2, COARSE, fine[:, :length]))
    for low, high, left in spans:
        out = dot(left, near[low * width : high * width, :])
        for k in range(low, high):
            raw[k, : left.shape[0], :] = out[:, (k - low) * width : (k - low + 1) * width]


def score(raw, factor, z):
    rows = factor.shape[0]
    width = factor.shape[1]
    for x in range(rows):
        each = jnp.broadcast_to(factor[x : x + 1, :], (FINE, width))
        pieces = [raw[k, pl.ds(x, FINE, stride=rows), :] * each for k in range(COARSE)]
        last = raw[COARSE - 1, pl.ds(FINE * rows + x, 1), :]
        edge = jnp.broadcast_to(last, (FINE, width)) * each
        z[:, x * width : (x + 1) * width] = jnp.concatenate(pieces + [edge, edge], 0).astype(BF16)


def gather_bins(z, table, acc):
    rows, width = table.shape
    ids = lax.broadcasted_iota(jnp.int32, (NB, width), 0).astype(F32)
    hots = []
    for x in range(rows):
        hit = jnp.broadcast_to(table[x : x + 1, :], (NB, width)) == ids
        hots.append(jnp.where(hit, 1.0, 0.0).astype(BF16))
    acc[...] += dot(jnp.concatenate(hots, 1), z[...])


def kernel(
    n_chan, n_seg, x_ref, b_ref, o_ref,
    cbuf, xbuf, nbuf, near_c, near_n, fine, raw, z, e_out, e_in, b_out, b_cross, b_near,
    t_fwd, t_rev, t_two, f_one, f_two, acc_fwd, acc_rev, acc_two, part, arrived, mine, others,
    e_send, e_recv, c_sem, x_send, x_recv, w_send, w_recv, n_send, n_recv, b_send, b_recv, r_send, r_recv, s_send, s_recv,
):
    channels, length = x_ref.shape
    half = channels // 2
    size = half // 2
    chan, seg = lax.axis_index("chan"), lax.axis_index("seg")
    loop = n_chan // 2
    side = chan // loop
    q = chan - side * loop
    parity = lax.rem(seg, 2)
    twin = seg + 1 - 2 * parity
    holder = parity == side
    helper = parity != side
    across = lax.rem(chan + loop, n_chan)
    above = side * loop + lax.rem(q + 1, loop)
    below = side * loop + lax.rem(q + loop - 1, loop)
    base = pl.multiple_of(half * jnp.where(holder, 1, 0), size)
    other_base = pl.multiple_of(half - base, size)
    wrap = (holder & (q == 0)) | (helper & (q == loop - 1))

    def send(src, dst, s_sem, r_sem, device):
        return pltpu.make_async_remote_copy(
            src_ref=src, dst_ref=dst, send_sem=s_sem, recv_sem=r_sem, device_id=device, device_id_type=MESH
        )

    barrier = pltpu.get_barrier_semaphore()
    peers = [(lax.rem(chan + k, n_chan), seg) for k in range(1, n_chan)]
    for k in range(1, n_seg):
        to = lax.rem(seg + k, n_seg)
        peers += [(chan, to), (across, to), (above, to), (below, to)]
    for peer in peers:
        pl.semaphore_signal(barrier, inc=1, device_id=peer, device_id_type=MESH)

    squares = jnp.zeros((channels, LANES), F32)
    for t in range(0, length, LANES):
        squares += jnp.square(x_ref[:, t : t + LANES].astype(F32))
    own_energy = jnp.sum(squares.T, axis=0, keepdims=True)
    e_out[...] = own_energy
    e_in[0, seg] = own_energy
    b_out[...] = b_ref[...].astype(F32).astype(BF16)
    t_fwd[...] = b_ref[0].astype(F32).T

    @pl.when(holder)
    def _():
        near_shifts(x_ref, near_c)

    acc_fwd[...] = jnp.zeros_like(acc_fwd)
    acc_rev[...] = jnp.zeros_like(acc_rev)
    acc_two[...] = jnp.zeros_like(acc_two)
    pl.semaphore_wait(barrier, len(peers))

    e_copies = []
    for k in range(1, n_seg):
        to = lax.rem(seg + k, n_seg)
        e_copies.append(send(e_out, e_in.at[0, seg], e_send.at[0, k], e_recv.at[0, k], (chan, to)))
    for k in range(n_seg):
        to = lax.rem(seg + k, n_seg)
        e_copies.append(send(e_out, e_in.at[1, seg], e_send.at[1, k], e_recv.at[1, k], (across, to)))
    for k in range(n_seg // 2):
        to = lax.rem(2 * k + side + seg - parity, n_seg)
        to_helper = lax.rem(2 * k + 1 - side + seg - parity, n_seg)
        e_copies.append(send(e_out, e_in.at[2, seg], e_send.at[2, k], e_recv.at[2, 2 * k + parity], (above, to)))
        e_copies.append(send(e_out, e_in.at[2, seg], e_send.at[3, k], e_recv.at[2, 2 * k + parity], (below, to_helper)))
    for copy in e_copies:
        copy.start()

    def cross_rows(start):
        return pl.ds(pl.multiple_of(start, size), size)

    def cross(i, to_holder):
        rows = cross_rows(i * size + (half if to_holder else 0))
        return send(x_ref.at[rows], xbuf.at[rows], x_send.at[i, to_holder], x_recv.at[i], (across, seg if to_holder else twin))

    to_twin = send(x_ref, cbuf, c_sem.at[0], c_sem.at[1], (chan, twin))
    to_above = send(x_ref, nbuf, n_send.at[0], n_recv.at[0], (above, seg))
    to_below = send(x_ref, nbuf, n_send.at[1], n_recv.at[0], (below, twin))
    to_wrap = send(x_ref, nbuf, n_send.at[1], n_recv.at[0], (below, seg))
    bins_zero = send(b_out.at[0, pl.ds(0, half)], b_cross, b_send.at[0], b_recv.at[0], (across, seg))
    bins_half = send(b_out.at[0, pl.ds(half, half)], b_cross, b_send.at[1], b_recv.at[0], (across, twin))
    bins_one = send(b_out.at[1], b_near, b_send.at[2], b_recv.at[1], (across, twin))
    bins_below = send(b_out.at[1], b_near, b_send.at[3], b_recv.at[1], (below, twin))
    from_holder = (to_twin, to_above, bins_zero, bins_half, bins_one, bins_below)

    @pl.when(holder)
    def _():
        to_twin.start()
        for copy in (bins_zero, bins_half, bins_one, bins_below):
            copy.start()
        to_above.start()

        @pl.when(q != 0)
        def _():
            to_below.start()

    @pl.when(helper)
    def _():
        for i in range(2):
            cross(i, 1).start()
            cross(i, 0).start()

        @pl.when(q == 0)
        def _():
            to_wrap.start()

        to_twin.wait_recv()
        near_shifts(cbuf, near_c)

    for k in range(1, n_seg):
        send(e_out, e_in.at[0, 0], e_send.at[0, k], e_recv.at[0, k], (chan, seg)).wait_recv()
    for k in range(n_seg):
        send(e_out, e_in.at[1, 0], e_send.at[1, k], e_recv.at[1, k], (chan, seg)).wait_recv()
        send(e_out, e_in.at[2, 0], e_send.at[2, 0], e_recv.at[2, k], (chan, seg)).wait_recv()
    total_time = length * n_seg

    def scale(slot):
        energy = e_in[slot, 0]
        for s in range(1, n_seg):
            energy = energy + e_in[slot, s]
        return lax.rsqrt(energy * (1.0 / total_time) + EPSILON)

    own, cross_scale, next_scale = scale(0), scale(1), scale(2)
    time_scale = 1.0 / math.sqrt(total_time)
    cross_column = jnp.broadcast_to(cross_scale, (channels, channels)).T
    f_one[...] = cross_column * own * time_scale
    centre_scale = jnp.where(wrap, own, cross_scale)
    f_two[...] = jnp.broadcast_to(centre_scale, (channels, channels)).T * next_scale * time_scale
    for copy in (bins_zero, bins_one):
        copy.wait_recv()
    t_rev[...] = b_cross[...].astype(F32)

    @pl.when(helper)
    def _():
        t_two[...] = b_near[...].astype(F32).T

    @pl.when(holder & (q != 0))
    def _():
        t_two[...] = b_near[...].astype(F32)

    @pl.when(holder & (q == 0))
    def _():
        t_two[...] = b_ref[1].astype(F32)

    def forward(i, start):
        rows = cross_rows(start + i * size)
        return send(xbuf.at[rows], xbuf.at[rows], w_send.at[i], w_recv.at[i], (chan, twin))

    for i in range(2):
        rows = cross_rows(base + i * size)
        cross(i, 1).wait_recv()
        forward(i, base).start()
        centre_shifts(xbuf[rows, :], fine)
        correlate(fine, near_c, raw)
        score(raw, f_one[rows, :], z)
        gather_bins(z, t_fwd[rows, :], acc_fwd)
        gather_bins(z, t_rev[pl.ds(i * size, size), :], acc_rev)

    to_above.wait_recv()
    near_shifts(nbuf, near_n)
    for i in range(4):
        start = (base if i < 2 else other_base) + (i % 2) * size
        rows = cross_rows(start)
        if i >= 2:
            forward(i - 2, base).wait_recv()

        @pl.when(wrap)
        def _():
            centre_shifts(x_ref[rows, :], fine)

        @pl.when(jnp.logical_not(wrap))
        def _():
            centre_shifts(xbuf[rows, :], fine)

        correlate(fine, near_n, raw)
        score(raw, f_two[rows, :], z)
        gather_bins(z, t_two[rows, :], acc_two)

    flip = lax.broadcasted_iota(jnp.int32, (ROWS, ROWS), 0) + lax.broadcasted_iota(jnp.int32, (ROWS, ROWS), 1)
    flip = jnp.where(flip == 2 * MAX_LAG, 1.0, 0.0).astype(F32)
    two = acc_two[...]
    ahead = acc_fwd[...] + jnp.where(holder, 0.0, two)
    back = acc_rev[...] + jnp.where(holder, two, 0.0)
    turned = lax.dot_general(
        back, flip, (((1,), (0,)), ((), ())), precision=lax.Precision.HIGHEST, preferred_element_type=F32
    )
    pair_total = ROUNDS * n_chan * channels * channels // NB
    part[...] = jnp.zeros_like(part)
    part[:, :ROWS] = (ahead + turned) * (1.0 / math.sqrt(pair_total))

    owned = part.shape[0] // n_chan
    first = []
    for k in range(1, n_chan):
        peer = lax.rem(chan + k, n_chan)
        src = part.at[pl.ds(pl.multiple_of(peer * owned, owned), owned)]
        copy = send(src, arrived.at[k - 1], r_send.at[k - 1], r_recv.at[k - 1], (peer, seg))
        copy.start()
        first.append(copy)
    running = part[pl.ds(pl.multiple_of(chan * owned, owned), owned), :]
    for k, copy in enumerate(first):
        copy.wait_recv()
        running = running + arrived[k]
    mine[...] = running
    others[seg] = running
    second = []
    for k in range(1, n_seg):
        copy = send(mine, others.at[seg], s_send.at[k], s_recv.at[k], (chan, lax.rem(seg + k, n_seg)))
        copy.start()
        second.append(copy)
    for copy in second:
        copy.wait_recv()
    sums = others[0]
    for s in range(1, n_seg):
        sums = sums + others[s]
    o_ref[...] = sums.T[:LAGS, :]

    for copy in e_copies + first + second:
        copy.wait_send()
    for i in range(2):
        forward(i, base).wait_send()

    @pl.when(holder)
    def _():
        for copy in from_holder:
            copy.wait_send()

        @pl.when(q != 0)
        def _():
            to_below.wait_send()

    @pl.when(helper)
    def _():
        for i in range(2):
            cross(i, 1).wait_send()
            cross(i, 0).wait_send()

        @pl.when(q == 0)
        def _():
            to_wrap.wait_send()


def local(traces, pair_bins):
    channels, length = traces.shape
    n_chan, n_seg = lax.axis_size("chan"), lax.axis_size("seg")
    size = channels // 4
    owned = NB // n_chan
    dma = pltpu.SemaphoreType.DMA
    block = pltpu.VMEM((channels, length), BF16)
    square = pltpu.VMEM((channels, channels), F32)
    stacked = pltpu.VMEM((NB, ROWS), F32)
    return pl.pallas_call(
        functools.partial(kernel, n_chan, n_seg),
        out_shape=jax.ShapeDtypeStruct((LAGS, owned), F32),
        in_specs=[pl.BlockSpec(memory_space=pltpu.VMEM)] * 2,
        out_specs=pl.BlockSpec(memory_space=pltpu.VMEM),
        scratch_shapes=[
            block, block, block,
            pltpu.VMEM((COARSE * channels, length), BF16),
            pltpu.VMEM((COARSE * channels, length), BF16),
            pltpu.VMEM(((FINE + 1) * size, length + LANES), BF16),
            pltpu.VMEM((COARSE, (FINE + 1) * size, channels), F32),
            pltpu.VMEM((ROWS, size * channels), BF16),
            pltpu.VMEM((1, channels), F32),
            pltpu.VMEM((3, n_seg, 1, channels), F32),
            pltpu.VMEM((2, channels, channels), BF16),
            pltpu.VMEM((channels // 2, channels), BF16),
            pltpu.VMEM((channels, channels), BF16),
            square, pltpu.VMEM((channels // 2, channels), F32), square, square, square,
            stacked, stacked, stacked,
            pltpu.VMEM((NB, LANES), F32),
            pltpu.VMEM((n_chan - 1, owned, LANES), F32),
            pltpu.VMEM((owned, LANES), F32),
            pltpu.VMEM((n_seg, owned, LANES), F32),
            dma((4, n_seg)), dma((3, n_seg)), dma((2,)), dma((2, 2)), dma((2,)), dma((2,)), dma((2,)),
            dma((2,)), dma((1,)), dma((4,)), dma((2,)),
            dma((n_chan - 1,)), dma((n_chan - 1,)), dma((n_seg,)), dma((n_seg,)),
        ],
        compiler_params=pltpu.CompilerParams(
            collective_id=0, has_side_effects=True, vmem_limit_bytes=48 * 1024 * 1024
        ),
    )(traces, pair_bins)


def solution(mesh):
    in_specs = (P("chan", "seg"), P(None, "chan", None))
    out_specs = P(None, "chan")
    return jax.shard_map(local, mesh=mesh, in_specs=in_specs, out_specs=out_specs, check_vma=False)
```

time: 64.4 us -> 48.9 us (0.76)
  Pallas kernels: 27.3 us -> 46.1 us
  starting transfers between devices: 14.5 us -> 0 us
  waiting for transfers between devices: 6.73 us -> 0 us
  blocking collectives: 6.59 us -> 0 us
  local copies, waits for them, and re-layouts: 5.88 us -> 2.63 us
  other arithmetic: 2.85 us -> 0 us
    pallas_call x5 -> x1, Pallas kernels: 27.3 us -> 46.1 us  [local(): pl.pallas_call(functools.partial(kernel, n_chan, n_seg), out_shape=jax.Sh...]
    ppermute x8 -> x0, starting transfers between devices: 14.5 us -> none  [from_behind(): return lax.ppermute(block, axis, route)]
    ppermute x8 -> x0, waiting for transfers between devices: 6.73 us -> none  [from_behind(): return lax.ppermute(block, axis, route)]
    psum x1 -> x0, blocking collectives: 6.59 us -> none  [local(): lax.psum(jnp.sum(jnp.square(traces.astype(jnp.float32)), axis=1), 'seg')]
    slice x4 -> x0, local copies, waits for them, and re-layouts: 2.03 us -> none  [the longest x1 1.13 us: local(): traces[k * size:(k + 1) * size]]
    concatenate x2 -> x0, other arithmetic: 1.48 us -> none  [the longest x1 1.47 us: local(): near = coarse_shifts(jnp.concatenate([traces, next_block], 0))]
    reduce_sum x1 -> x0, other arithmetic: 1.26 us -> none  [local(): jnp.sum(jnp.square(traces.astype(jnp.float32)), axis=1)]
    unnamed x12 -> x4, local copies, waits for them, and re-layouts: 2.67 us -> 1.94 us
  transfers between devices with their start and end apart: 8 -> 0, of which waited for: 1 -> 0; matrix products, arithmetic and copies ran while one was open for 12% -> 0% of each run, Pallas kernels for 21% -> 0%
where the time goes in v1:
time: 48.9 us; the launch traced here: 48.7 us
  Pallas kernels  46.1 us (94%)
  local copies, waits for them, and re-layouts  2.63 us (5%)
    pallas_call x1, Pallas kernels, local(): pl.pallas_call(functools.partial(kernel, n_chan, n_seg), out_shape=jax.Sh...  46.1 us
    unnamed x4, local copies, waits for them, and re-layouts  1.94 us

profile of v1, /device:TPU:0, one launch (start us, length us, event | category | flops | bytes accessed | tf_op | source)
XLA Modules:
  0.0 48.7 jit_solution(2525197372273120784)
XLA Ops:
  0.0 0.0 copy-start
  0.0 1.0 %copy-done = bf16[128,2048]{1,0:T(8,128)(2,1)S(1)} copy-done((bf16[128,2048]{1,0:T(8,128)(2,1)S(1)}, bf16[128,2048]{1,0:T(8,128)(2,1)}, u32[]{:S(2)}) %copy-start) | copy-done | bytes 524312
  1.0 0.0 copy-start.1
  1.0 0.9 %copy-done.1 = s32[2,128,128]{2,1,0:T(8,128)S(1)} copy-done((s32[2,128,128]{2,1,0:T(8,128)S(1)}, s32[2,128,128]{2,1,0:T(8,128)}, u32[]{:S(2)}) %copy-start.1) | copy-done | bytes 131096
  1.9 46.1 %shard_map.28 = f32[65,32]{1,0:T(8,128)S(1)} custom-call(bf16[128,2048]{1,0:T(8,128)(2,1)S(1)} %copy-done, s32[2,128,128]{2,1,0:T(8,128)S(1)} %copy-done.1), custom_call_target="tpu_custom_call" | custom-call | tf_op jit(solution)/shard_map/pallas_call | solution.py:358
  48.1 0.7 %copy.3 = f32[65,32]{0,1:T(8,128)} copy(f32[65,32]{1,0:T(8,128)S(1)} %shard_map.28) | data formatting | bytes 16640 | tf_op jit(solution)/shard_map/pallas_call | solution.py:358
Async XLA Ops:
  0.0 1.0 %copy-start = (bf16[128,2048]{1,0:T(8,128)(2,1)S(1)}, bf16[128,2048]{1,0:T(8,128)(2,1)}, u32[]{:S(2)}) copy-start(bf16[128,2048]{1,0:T(8,128)(2,1)} %x_ref.1) | copy-start | bytes 1572868
  1.0 0.9 %copy-start.1 = (s32[2,128,128]{2,1,0:T(8,128)S(1)}, s32[2,128,128]{2,1,0:T(8,128)}, u32[]{:S(2)}) copy-start(s32[2,128,128]{2,1,0:T(8,128)} %b_ref.1) | copy-start | bytes 393220

commit v2 on v1

--- a/solution.py
+++ b/solution.py
@@ -18,98 +18,142 @@
 COARSE = 2 * MAX_LAG // FINE
 LANES = 128
 ROWS = 80
+TILE = 16
+GROUP = 8
 MESH = pl.DeviceIdType.MESH
 CONTRACT = (((1,), (1,)), ((), ()))
 F32, BF16 = jnp.float32, jnp.bfloat16
 
+NEAR = MAX_LAG - FINE
+SPAN = FINE
+
 
 def dot(left, right):
     return lax.dot_general(left, right, CONTRACT, preferred_element_type=F32)
 
 
-def lane_mask(rows, low, high):
-    lane = lax.broadcasted_iota(jnp.int32, (rows, LANES), 1)
-    return jnp.where((lane >= low) & (lane < high), 1.0, 0.0).astype(BF16)
-
-
-def near_shifts(source, shifted):
+def lanes(rows):
+    return lax.broadcasted_iota(jnp.int32, (rows, LANES), 1)
+
+
+def columns_first(cols):
+    count = len(cols)
+    lane = lanes(cols[0].shape[0])
+    step = 1
+    while step < count:
+        bit = (lane & step) != 0
+        done = list(cols)
+        for u in range(count):
+            if not u & step:
+                low, high = cols[u], cols[u + step]
+                done[u] = jnp.where(bit, pltpu.roll(high, step, 1), low)
+                done[u + step] = jnp.where(bit, high, pltpu.roll(low, LANES - step, 1))
+        cols = done
+        step *= 2
+    return cols
+
+
+def later(col, count):
+    lane = lanes(col.shape[0])
+    inner = pltpu.roll(col, LANES - count, 1)
+    outer = jnp.where(lane < LANES - 1, pltpu.roll(col, LANES - count - 1, 1), 0.0)
+    return jnp.where(lane < LANES - count, inner, outer)
+
+
+def earlier(col, count):
+    lane = lanes(col.shape[0])
+    inner = pltpu.roll(col, count, 1)
+    outer = jnp.where(lane > 0, pltpu.roll(col, count + 1, 1), 0.0)
+    return jnp.where(lane >= count, inner, outer)
+
+
+def at(column):
+    return slice(column * LANES, (column + 1) * LANES)
+
+
+def beside(load, store, count, low, high):
+    for i in range(count):
+        col = None
+        for c in range(i + count, count + high, count):
+            col = later(load(i) if col is None else col, count)
+            store(c, col)
+        col = None
+        for c in range(i - count, -low - 1, -count):
+            col = earlier(load(i) if col is None else col, count)
+            store(c, col)
+
+
+def spread_near(source, wide):
     rows, length = source.shape
-    block = source[...]
-    for k in range(COARSE):
-        step = FINE * (k - COARSE // 2)
-        at = slice(k * rows, (k + 1) * rows)
-        if step == 0:
-            shifted[at, :] = block
-            continue
-        turned = pltpu.roll(block, step % length, 1)
-        if step > 0:
-            shifted[at, :LANES] = turned[:, :LANES] * lane_mask(rows, step, LANES)
-            shifted[at, LANES:] = turned[:, LANES:]
-        else:
-            keep = 1 - lane_mask(rows, LANES + step, LANES - FINE)
-            shifted[at, : length - LANES] = turned[:, : length - LANES]
-            shifted[at, length - LANES :] = turned[:, length - LANES :] * keep
-
-
-def centre_shifts(block, fine):
-    rows, length = block.shape
-    for f in range(FINE + 1):
-        at = slice(f * rows, (f + 1) * rows)
-        if f == 0:
-            fine[at, :length] = block
-            fine[at, length:] = block[:, length - LANES :] * lane_mask(rows, 0, LANES - FINE)
-            continue
-        turned = pltpu.roll(block, length - f, 1)
-        tail = turned[:, length - LANES :]
-        fine[at, : length - LANES] = turned[:, : length - LANES]
-        fine[at, length - LANES : length] = tail * lane_mask(rows, 0, LANES - f)
-        if f < FINE:
-            fine[at, length:] = tail * (1 - lane_mask(rows, LANES - FINE, LANES - f))
-
-
-def correlate(fine, near, raw):
-    width = near.shape[0] // COARSE
-    length = near.shape[1]
-    total = fine.shape[0]
-    rows = total // (FINE + 1)
-    plain = FINE * rows
-    wrapped = jnp.concatenate([fine[:plain, : length - LANES], fine[:plain, length:]], 1)
-    half = COARSE // 2
-    spans = ((0, half, wrapped), (half, COARSE - 2, fine[:plain, :length]), (COARSE - 2, COARSE, fine[:, :length]))
-    for low, high, left in spans:
-        out = dot(left, near[low * width : high * width, :])
-        for k in range(low, high):
-            raw[k, : left.shape[0], :] = out[:, (k - low) * width : (k - low + 1) * width]
-
-
-def score(raw, factor, z):
-    rows = factor.shape[0]
+    count = length // LANES
+
+    @pl.loop(0, rows // TILE)
+    def _(g):
+        here = pl.ds(pl.multiple_of(g * TILE, TILE), TILE)
+        wide[here, NEAR * LANES : NEAR * LANES + length] = source[here, :]
+
+        def store(c, col):
+            wide[here, at(NEAR + c)] = col.astype(BF16)
+
+        beside(lambda i: source[here, at(i)].astype(F32), store, count, NEAR, NEAR)
+
+
+def spread_centre(block, start, rows, count):
+    @pl.loop(0, rows // TILE)
+    def _(g):
+        here = pl.ds(pl.multiple_of(start + g * TILE, TILE), TILE)
+
+        def store(c, col):
+            block[here, at(SPAN + c)] = col.astype(BF16)
+
+        beside(lambda i: block[here, at(SPAN + i)].astype(F32), store, count, SPAN, SPAN)
+
+
+def correlate(centre, near, raw, piece):
+    rows, span = centre.shape
+    length = span - 2 * SPAN * LANES
+    pair = 2
+    steps = FINE + 1 if piece == COARSE // pair - 1 else FINE
+    first = 0 if piece < COARSE // pair // 2 else SPAN
+    left = [centre[:, (first + f) * LANES : (first + f) * LANES + length] for f in range(steps)]
+    right = []
+    for k in range(pair * piece, pair * piece + pair):
+        column = NEAR - FINE * (k - COARSE // 2) - (FINE if k < COARSE // 2 else 0)
+        right.append(near[:, column * LANES : column * LANES + length])
+    out = dot(jnp.concatenate(left, 0), jnp.concatenate(right, 0))
+    width = near.shape[0]
+    for k in range(pair):
+        raw[pair * piece + k, : steps * rows, :] = out[:, k * width : (k + 1) * width]
+
+
+def bin_rows(raw, rows, group, factor, targets):
     width = factor.shape[1]
-    for x in range(rows):
+    scores = []
+    for x in range(group * GROUP, (group + 1) * GROUP):
         each = jnp.broadcast_to(factor[x : x + 1, :], (FINE, width))
         pieces = [raw[k, pl.ds(x, FINE, stride=rows), :] * each for k in range(COARSE)]
         last = raw[COARSE - 1, pl.ds(FINE * rows + x, 1), :]
         edge = jnp.broadcast_to(last, (FINE, width)) * each
-        z[:, x * width : (x + 1) * width] = jnp.concatenate(pieces + [edge, edge], 0).astype(BF16)
-
-
-def gather_bins(z, table, acc):
-    rows, width = table.shape
-    ids = lax.broadcasted_iota(jnp.int32, (NB, width), 0).astype(F32)
-    hots = []
-    for x in range(rows):
-        hit = jnp.broadcast_to(table[x : x + 1, :], (NB, width)) == ids
-        hots.append(jnp.where(hit, 1.0, 0.0).astype(BF16))
-    acc[...] += dot(jnp.concatenate(hots, 1), z[...])
+        scores.append(jnp.concatenate(pieces + [edge, edge], 0).astype(BF16))
+    score = jnp.concatenate(scores, 1)
+    ids = lax.broadcasted_iota(jnp.int32, (NB, width), 0).astype(F32).astype(BF16)
+    one, none = jnp.asarray(1, BF16), jnp.asarray(0, BF16)
+    for table, acc in targets:
+        hots = []
+        for x in range(group * GROUP, (group + 1) * GROUP):
+            hit = jnp.broadcast_to(table[x : x + 1, :].astype(BF16), (NB, width)) == ids
+            hots.append(jnp.where(hit, one, none))
+        acc[...] += dot(jnp.concatenate(hots, 1), score)
 
 
 def kernel(
     n_chan, n_seg, x_ref, b_ref, o_ref,
-    cbuf, xbuf, nbuf, near_c, near_n, fine, raw, z, e_out, e_in, b_out, b_cross, b_near,
-    t_fwd, t_rev, t_two, f_one, f_two, acc_fwd, acc_rev, acc_two, part, arrived, mine, others,
+    trace, bins, cbuf, centres, nbuf, near_c, near_n, raw, i_sem, e_out, e_in, b_out, b_cross, b_near,
+    t_fwd, t_rev, t_two, f_one, f_two, acc_fwd, acc_rev, acc_two, squares, part, arrived, mine, others,
     e_send, e_recv, c_sem, x_send, x_recv, w_send, w_recv, n_send, n_recv, b_send, b_recv, r_send, r_recv, s_send, s_recv,
 ):
-    channels, length = x_ref.shape
+    channels, length = trace.shape
+    count = length // LANES
     half = channels // 2
     size = half // 2
     chan, seg = lax.axis_index("chan"), lax.axis_index("seg")
@@ -132,6 +176,12 @@
             src_ref=src, dst_ref=dst, send_sem=s_sem, recv_sem=r_sem, device_id=device, device_id_type=MESH
         )
 
+    bins_in = pltpu.make_async_copy(b_ref, bins, i_sem.at[0])
+    trace_in = pltpu.make_async_copy(x_ref, trace, i_sem.at[1])
+    trace_in.start()
+    bins_in.start()
+    xbuf = centres.at[0, :, pl.ds(SPAN * LANES, length)]
+    own = centres.at[1, :, pl.ds(SPAN * LANES, length)]
     barrier = pltpu.get_barrier_semaphore()
     peers = [(lax.rem(chan + k, n_chan), seg) for k in range(1, n_chan)]
     for k in range(1, n_seg):
@@ -140,19 +190,26 @@
     for peer in peers:
         pl.semaphore_signal(barrier, inc=1, device_id=peer, device_id_type=MESH)
 
-    squares = jnp.zeros((channels, LANES), F32)
-    for t in range(0, length, LANES):
-        squares += jnp.square(x_ref[:, t : t + LANES].astype(F32))
-    own_energy = jnp.sum(squares.T, axis=0, keepdims=True)
+    bins_in.wait()
+    b_out[...] = bins[...].astype(F32).astype(BF16)
+    t_fwd[...] = bins[0].astype(F32).T
+    trace_in.wait()
+    squares[...] = jnp.zeros_like(squares)
+
+    @pl.loop(0, channels // TILE)
+    def _(g):
+        here = pl.ds(pl.multiple_of(g * TILE, TILE), TILE)
+        cols = [trace[here, at(i)].astype(F32) for i in range(count)]
+        total = jnp.square(cols[0])
+        for col in cols[1:]:
+            total += jnp.square(col)
+        squares[here, :] = total
+        for i, col in enumerate(columns_first(cols)):
+            own[here, at(i)] = col.astype(BF16)
+
+    own_energy = jnp.sum(squares[...].T, axis=0, keepdims=True)
     e_out[...] = own_energy
     e_in[0, seg] = own_energy
-    b_out[...] = b_ref[...].astype(F32).astype(BF16)
-    t_fwd[...] = b_ref[0].astype(F32).T
-
-    @pl.when(holder)
-    def _():
-        near_shifts(x_ref, near_c)
-
     acc_fwd[...] = jnp.zeros_like(acc_fwd)
     acc_rev[...] = jnp.zeros_like(acc_rev)
     acc_two[...] = jnp.zeros_like(acc_two)
@@ -178,12 +235,12 @@
 
     def cross(i, to_holder):
         rows = cross_rows(i * size + (half if to_holder else 0))
-        return send(x_ref.at[rows], xbuf.at[rows], x_send.at[i, to_holder], x_recv.at[i], (across, seg if to_holder else twin))
-
-    to_twin = send(x_ref, cbuf, c_sem.at[0], c_sem.at[1], (chan, twin))
-    to_above = send(x_ref, nbuf, n_send.at[0], n_recv.at[0], (above, seg))
-    to_below = send(x_ref, nbuf, n_send.at[1], n_recv.at[0], (below, twin))
-    to_wrap = send(x_ref, nbuf, n_send.at[1], n_recv.at[0], (below, seg))
+        return send(own.at[rows], xbuf.at[rows], x_send.at[i, to_holder], x_recv.at[i], (across, seg if to_holder else twin))
+
+    to_twin = send(own, cbuf, c_sem.at[0], c_sem.at[1], (chan, twin))
+    to_above = send(own, nbuf, n_send.at[0], n_recv.at[0], (above, seg))
+    to_below = send(own, nbuf, n_send.at[1], n_recv.at[0], (below, twin))
+    to_wrap = send(own, nbuf, n_send.at[1], n_recv.at[0], (below, seg))
     bins_zero = send(b_out.at[0, pl.ds(0, half)], b_cross, b_send.at[0], b_recv.at[0], (across, seg))
     bins_half = send(b_out.at[0, pl.ds(half, half)], b_cross, b_send.at[1], b_recv.at[0], (across, twin))
     bins_one = send(b_out.at[1], b_near, b_send.at[2], b_recv.at[1], (across, twin))
@@ -201,6 +258,8 @@
         def _():
             to_below.start()
 
+        spread_near(own, near_c)
+
     @pl.when(helper)
     def _():
         for i in range(2):
@@ -212,7 +271,7 @@
             to_wrap.start()
 
         to_twin.wait_recv()
-        near_shifts(cbuf, near_c)
+        spread_near(cbuf, near_c)
 
     for k in range(1, n_seg):
         send(e_out, e_in.at[0, 0], e_send.at[0, k], e_recv.at[0, k], (chan, seg)).wait_recv()
@@ -227,11 +286,11 @@
             energy = energy + e_in[slot, s]
         return lax.rsqrt(energy * (1.0 / total_time) + EPSILON)
 
-    own, cross_scale, next_scale = scale(0), scale(1), scale(2)
+    own_scale, cross_scale, next_scale = scale(0), scale(1), scale(2)
     time_scale = 1.0 / math.sqrt(total_time)
     cross_column = jnp.broadcast_to(cross_scale, (channels, channels)).T
-    f_one[...] = cross_column * own * time_scale
-    centre_scale = jnp.where(wrap, own, cross_scale)
+    f_one[...] = cross_column * own_scale * time_scale
+    centre_scale = jnp.where(wrap, own_scale, cross_scale)
     f_two[...] = jnp.broadcast_to(centre_scale, (channels, channels)).T * next_scale * time_scale
     for copy in (bins_zero, bins_one):
         copy.wait_recv()
@@ -247,41 +306,47 @@
 
     @pl.when(holder & (q == 0))
     def _():
-        t_two[...] = b_ref[1].astype(F32)
+        t_two[...] = bins[1].astype(F32)
 
     def forward(i, start):
         rows = cross_rows(start + i * size)
         return send(xbuf.at[rows], xbuf.at[rows], w_send.at[i], w_recv.at[i], (chan, twin))
 
+    pieces = size // GROUP
+
+    def advance(i, centre, near, after):
+        for p in range(pieces):
+            if centre is not None:
+                correlate(centre, near, raw.at[i % 2], p)
+            if after is not None:
+                bin_rows(raw.at[(i + 1) % 2], size, p, *after)
+
+    after = None
     for i in range(2):
         rows = cross_rows(base + i * size)
         cross(i, 1).wait_recv()
         forward(i, base).start()
-        centre_shifts(xbuf[rows, :], fine)
-        correlate(fine, near_c, raw)
-        score(raw, f_one[rows, :], z)
-        gather_bins(z, t_fwd[rows, :], acc_fwd)
-        gather_bins(z, t_rev[pl.ds(i * size, size), :], acc_rev)
-
+        spread_centre(centres.at[0], base + i * size, size, count)
+        advance(i, centres.at[0, rows], near_c, after)
+        late = pl.ds(i * size, size)
+        after = (f_one.at[rows], ((t_fwd.at[rows], acc_fwd), (t_rev.at[late], acc_rev)))
+
+    @pl.when(wrap)
+    def _():
+        spread_centre(centres.at[1], 0, channels, count)
+
+    chosen = jnp.where(wrap, 1, 0)
     to_above.wait_recv()
-    near_shifts(nbuf, near_n)
+    spread_near(nbuf, near_n)
     for i in range(4):
         start = (base if i < 2 else other_base) + (i % 2) * size
         rows = cross_rows(start)
         if i >= 2:
             forward(i - 2, base).wait_recv()
-
-        @pl.when(wrap)
-        def _():
-            centre_shifts(x_ref[rows, :], fine)
-
-        @pl.when(jnp.logical_not(wrap))
-        def _():
-            centre_shifts(xbuf[rows, :], fine)
-
-        correlate(fine, near_n, raw)
-        score(raw, f_two[rows, :], z)
-        gather_bins(z, t_two[rows, :], acc_two)
+            spread_centre(centres.at[0], start, size, count)
+        advance(i, centres.at[chosen, rows], near_n, after)
+        after = (f_two.at[rows], ((t_two.at[rows], acc_two),))
+    advance(4, None, None, after)
 
     flip = lax.broadcasted_iota(jnp.int32, (ROWS, ROWS), 0) + lax.broadcasted_iota(jnp.int32, (ROWS, ROWS), 1)
     flip = jnp.where(flip == 2 * MAX_LAG, 1.0, 0.0).astype(F32)
@@ -354,19 +419,21 @@
     dma = pltpu.SemaphoreType.DMA
     block = pltpu.VMEM((channels, length), BF16)
     square = pltpu.VMEM((channels, channels), F32)
+    wide = pltpu.VMEM((channels, length + 2 * NEAR * LANES), BF16)
     stacked = pltpu.VMEM((NB, ROWS), F32)
     return pl.pallas_call(
         functools.partial(kernel, n_chan, n_seg),
         out_shape=jax.ShapeDtypeStruct((LAGS, owned), F32),
-        in_specs=[pl.BlockSpec(memory_space=pltpu.VMEM)] * 2,
+        in_specs=[pl.BlockSpec(memory_space=pltpu.HBM)] * 2,
         out_specs=pl.BlockSpec(memory_space=pltpu.VMEM),
         scratch_shapes=[
-            block, block, block,
-            pltpu.VMEM((COARSE * channels, length), BF16),
-            pltpu.VMEM((COARSE * channels, length), BF16),
-            pltpu.VMEM(((FINE + 1) * size, length + LANES), BF16),
-            pltpu.VMEM((COARSE, (FINE + 1) * size, channels), F32),
-            pltpu.VMEM((ROWS, size * channels), BF16),
+            block,
+            pltpu.VMEM((2, channels, channels), jnp.int32),
+            block,
+            pltpu.VMEM((2, channels, length + 2 * SPAN * LANES), BF16),
+            block, wide, wide,
+            pltpu.VMEM((2, COARSE, (FINE + 1) * size, channels), F32),
+            dma((2,)),
             pltpu.VMEM((1, channels), F32),
             pltpu.VMEM((3, n_seg, 1, channels), F32),
             pltpu.VMEM((2, channels, channels), BF16),
@@ -374,6 +441,7 @@
             pltpu.VMEM((channels, channels), BF16),
             square, pltpu.VMEM((channels // 2, channels), F32), square, square, square,
             stacked, stacked, stacked,
+            pltpu.VMEM((channels, LANES), F32),
             pltpu.VMEM((NB, LANES), F32),
             pltpu.VMEM((n_chan - 1, owned, LANES), F32),
             pltpu.VMEM((owned, LANES), F32),

time: 48.9 us -> 47.7 us (0.975)
  Pallas kernels: 46.1 us -> 44.9 us
    pallas_call x1, Pallas kernels: 46.1 us -> 44.9 us  [local(): pl.pallas_call(functools.partial(kernel, n_chan, n_seg), out_shape=jax.Sh...]
where the time goes in v2:
time: 47.7 us; the launch traced here: 47.6 us
  Pallas kernels  44.9 us (94%)
  local copies, waits for them, and re-layouts  2.63 us (6%)
    pallas_call x1, Pallas kernels, local(): pl.pallas_call(functools.partial(kernel, n_chan, n_seg), out_shape=jax.Sh...  44.9 us
    unnamed x4, local copies, waits for them, and re-layouts  1.94 us

profile of v2, /device:TPU:0, one launch (start us, length us, event | category | flops | bytes accessed | tf_op | source)
XLA Modules:
  0.0 47.6 jit_solution(8256155134068805515)
XLA Ops:
  0.0 0.0 copy-start
  0.0 1.0 %copy-done = bf16[128,2048]{1,0:T(8,128)(2,1)S(1)} copy-done((bf16[128,2048]{1,0:T(8,128)(2,1)S(1)}, bf16[128,2048]{1,0:T(8,128)(2,1)}, u32[]{:S(2)}) %copy-start) | copy-done | bytes 524312
  1.0 0.0 copy-start.1
  1.0 0.9 %copy-done.1 = s32[2,128,128]{2,1,0:T(8,128)S(1)} copy-done((s32[2,128,128]{2,1,0:T(8,128)S(1)}, s32[2,128,128]{2,1,0:T(8,128)}, u32[]{:S(2)}) %copy-start.1) | copy-done | bytes 131096
  1.9 44.9 %shard_map.28 = f32[65,32]{1,0:T(8,128)S(1)} custom-call(bf16[128,2048]{1,0:T(8,128)(2,1)S(1)} %copy-done, s32[2,128,128]{2,1,0:T(8,128)S(1)} %copy-done.1), custom_call_target="tpu_custom_call" | custom-call | tf_op jit(solution)/shard_map/pallas_call | solution.py:424
  46.9 0.7 %copy.3 = f32[65,32]{0,1:T(8,128)} copy(f32[65,32]{1,0:T(8,128)S(1)} %shard_map.28) | data formatting | bytes 16640 | tf_op jit(solution)/shard_map/pallas_call | solution.py:424
Async XLA Ops:
  0.0 1.0 %copy-start = (bf16[128,2048]{1,0:T(8,128)(2,1)S(1)}, bf16[128,2048]{1,0:T(8,128)(2,1)}, u32[]{:S(2)}) copy-start(bf16[128,2048]{1,0:T(8,128)(2,1)} %x_ref.1) | copy-start | bytes 1572868
  1.0 0.9 %copy-start.1 = (s32[2,128,128]{2,1,0:T(8,128)S(1)}, s32[2,128,128]{2,1,0:T(8,128)}, u32[]{:S(2)}) copy-start(s32[2,128,128]{2,1,0:T(8,128)} %b_ref.1) | copy-start | bytes 393220

commit v3 on v2

--- a/solution.py
+++ b/solution.py
@@ -87,7 +87,7 @@
     rows, length = source.shape
     count = length // LANES
 
-    @pl.loop(0, rows // TILE)
+    @pl.loop(0, rows // TILE, unroll=True)
     def _(g):
         here = pl.ds(pl.multiple_of(g * TILE, TILE), TILE)
         wide[here, NEAR * LANES : NEAR * LANES + length] = source[here, :]
@@ -99,7 +99,7 @@
 
 
 def spread_centre(block, start, rows, count):
-    @pl.loop(0, rows // TILE)
+    @pl.loop(0, rows // TILE, unroll=True)
     def _(g):
         here = pl.ds(pl.multiple_of(start + g * TILE, TILE), TILE)
 
@@ -150,7 +150,7 @@
     n_chan, n_seg, x_ref, b_ref, o_ref,
     trace, bins, cbuf, centres, nbuf, near_c, near_n, raw, i_sem, e_out, e_in, b_out, b_cross, b_near,
     t_fwd, t_rev, t_two, f_one, f_two, acc_fwd, acc_rev, acc_two, squares, part, arrived, mine, others,
-    e_send, e_recv, c_sem, x_send, x_recv, w_send, w_recv, n_send, n_recv, b_send, b_recv, r_send, r_recv, s_send, s_recv,
+    e_send, e_recv, c_sem, x_send, x_recv, w_send, w_recv, n_send, n_recv, b_send, b_recv, r_send, r_recv, s_send, s_recv, known,
 ):
     channels, length = trace.shape
     count = length // LANES
@@ -183,7 +183,8 @@
     xbuf = centres.at[0, :, pl.ds(SPAN * LANES, length)]
     own = centres.at[1, :, pl.ds(SPAN * LANES, length)]
     barrier = pltpu.get_barrier_semaphore()
-    peers = [(lax.rem(chan + k, n_chan), seg) for k in range(1, n_chan)]
+    beside_us = [(across, seg), (above, seg), (below, seg)]
+    peers = list(beside_us)
     for k in range(1, n_seg):
         to = lax.rem(seg + k, n_seg)
         peers += [(chan, to), (across, to), (above, to), (below, to)]
@@ -192,11 +193,10 @@
 
     bins_in.wait()
     b_out[...] = bins[...].astype(F32).astype(BF16)
-    t_fwd[...] = bins[0].astype(F32).T
     trace_in.wait()
     squares[...] = jnp.zeros_like(squares)
 
-    @pl.loop(0, channels // TILE)
+    @pl.loop(0, channels // TILE, unroll=True)
     def _(g):
         here = pl.ds(pl.multiple_of(g * TILE, TILE), TILE)
         cols = [trace[here, at(i)].astype(F32) for i in range(count)]
@@ -214,6 +214,13 @@
     acc_rev[...] = jnp.zeros_like(acc_rev)
     acc_two[...] = jnp.zeros_like(acc_two)
     pl.semaphore_wait(barrier, len(peers))
+
+    def tell(i):
+        for peer in beside_us:
+            pl.semaphore_signal(known.at[i], inc=1, device_id=peer, device_id_type=MESH)
+
+    rounds = loop // 2
+    tell(0)
 
     e_copies = []
     for k in range(1, n_seg):
@@ -273,41 +280,6 @@
         to_twin.wait_recv()
         spread_near(cbuf, near_c)
 
-    for k in range(1, n_seg):
-        send(e_out, e_in.at[0, 0], e_send.at[0, k], e_recv.at[0, k], (chan, seg)).wait_recv()
-    for k in range(n_seg):
-        send(e_out, e_in.at[1, 0], e_send.at[1, k], e_recv.at[1, k], (chan, seg)).wait_recv()
-        send(e_out, e_in.at[2, 0], e_send.at[2, 0], e_recv.at[2, k], (chan, seg)).wait_recv()
-    total_time = length * n_seg
-
-    def scale(slot):
-        energy = e_in[slot, 0]
-        for s in range(1, n_seg):
-            energy = energy + e_in[slot, s]
-        return lax.rsqrt(energy * (1.0 / total_time) + EPSILON)
-
-    own_scale, cross_scale, next_scale = scale(0), scale(1), scale(2)
-    time_scale = 1.0 / math.sqrt(total_time)
-    cross_column = jnp.broadcast_to(cross_scale, (channels, channels)).T
-    f_one[...] = cross_column * own_scale * time_scale
-    centre_scale = jnp.where(wrap, own_scale, cross_scale)
-    f_two[...] = jnp.broadcast_to(centre_scale, (channels, channels)).T * next_scale * time_scale
-    for copy in (bins_zero, bins_one):
-        copy.wait_recv()
-    t_rev[...] = b_cross[...].astype(F32)
-
-    @pl.when(helper)
-    def _():
-        t_two[...] = b_near[...].astype(F32).T
-
-    @pl.when(holder & (q != 0))
-    def _():
-        t_two[...] = b_near[...].astype(F32)
-
-    @pl.when(holder & (q == 0))
-    def _():
-        t_two[...] = bins[1].astype(F32)
-
     def forward(i, start):
         rows = cross_rows(start + i * size)
         return send(xbuf.at[rows], xbuf.at[rows], w_send.at[i], w_recv.at[i], (chan, twin))
@@ -320,6 +292,43 @@
                 correlate(centre, near, raw.at[i % 2], p)
             if after is not None:
                 bin_rows(raw.at[(i + 1) % 2], size, p, *after)
+
+    def tables():
+        for k in range(1, n_seg):
+            send(e_out, e_in.at[0, 0], e_send.at[0, k], e_recv.at[0, k], (chan, seg)).wait_recv()
+        for k in range(n_seg):
+            send(e_out, e_in.at[1, 0], e_send.at[1, k], e_recv.at[1, k], (chan, seg)).wait_recv()
+            send(e_out, e_in.at[2, 0], e_send.at[2, 0], e_recv.at[2, k], (chan, seg)).wait_recv()
+        total_time = length * n_seg
+
+        def scale(slot):
+            energy = e_in[slot, 0]
+            for s in range(1, n_seg):
+                energy = energy + e_in[slot, s]
+            return lax.rsqrt(energy * (1.0 / total_time) + EPSILON)
+
+        own_scale, cross_scale, next_scale = scale(0), scale(1), scale(2)
+        time_scale = 1.0 / math.sqrt(total_time)
+        cross_column = jnp.broadcast_to(cross_scale, (channels, channels)).T
+        f_one[...] = cross_column * own_scale * time_scale
+        centre_scale = jnp.where(wrap, own_scale, cross_scale)
+        f_two[...] = jnp.broadcast_to(centre_scale, (channels, channels)).T * next_scale * time_scale
+        for copy in (bins_zero, bins_one):
+            copy.wait_recv()
+        t_fwd[...] = bins[0].astype(F32).T
+        t_rev[...] = b_cross[...].astype(F32)
+
+        @pl.when(helper)
+        def _():
+            t_two[...] = b_near[...].astype(F32).T
+
+        @pl.when(holder & (q != 0))
+        def _():
+            t_two[...] = b_near[...].astype(F32)
+
+        @pl.when(holder & (q == 0))
+        def _():
+            t_two[...] = bins[1].astype(F32)
 
     after = None
     for i in range(2):
@@ -328,6 +337,8 @@
         forward(i, base).start()
         spread_centre(centres.at[0], base + i * size, size, count)
         advance(i, centres.at[0, rows], near_c, after)
+        if i == 0:
+            tables()
         late = pl.ds(i * size, size)
         after = (f_one.at[rows], ((t_fwd.at[rows], acc_fwd), (t_rev.at[late], acc_rev)))
 
@@ -339,6 +350,10 @@
     to_above.wait_recv()
     spread_near(nbuf, near_n)
     for i in range(4):
+        if i < rounds:
+            pl.semaphore_wait(known.at[i], len(beside_us))
+            if i + 1 < rounds:
+                tell(i + 1)
         start = (base if i < 2 else other_base) + (i % 2) * size
         rows = cross_rows(start)
         if i >= 2:
@@ -346,6 +361,10 @@
             spread_centre(centres.at[0], start, size, count)
         advance(i, centres.at[chosen, rows], near_n, after)
         after = (f_two.at[rows], ((t_two.at[rows], acc_two),))
+    for i in range(4, rounds):
+        pl.semaphore_wait(known.at[i], len(beside_us))
+        if i + 1 < rounds:
+            tell(i + 1)
     advance(4, None, None, after)
 
     flip = lax.broadcasted_iota(jnp.int32, (ROWS, ROWS), 0) + lax.broadcasted_iota(jnp.int32, (ROWS, ROWS), 1)
@@ -449,9 +468,10 @@
             dma((4, n_seg)), dma((3, n_seg)), dma((2,)), dma((2, 2)), dma((2,)), dma((2,)), dma((2,)),
             dma((2,)), dma((1,)), dma((4,)), dma((2,)),
             dma((n_chan - 1,)), dma((n_chan - 1,)), dma((n_seg,)), dma((n_seg,)),
+            pltpu.SemaphoreType.REGULAR((n_chan // 4,)),
         ],
         compiler_params=pltpu.CompilerParams(
-            collective_id=0, has_side_effects=True, vmem_limit_bytes=48 * 1024 * 1024
+            collective_id=0, has_side_effects=True, vmem_limit_bytes=63 * 1024 * 1024
         ),
     )(traces, pair_bins)
 

time: 47.7 us -> 52.3 us (1.096)
  Pallas kernels: 44.9 us -> 50.7 us
  local copies, waits for them, and re-layouts: 2.63 us -> 1.45 us
    pallas_call x1, Pallas kernels: 44.9 us -> 50.7 us  [local(): pl.pallas_call(functools.partial(kernel, n_chan, n_seg), out_shape=jax.Sh...]
    unnamed x4 -> x0, local copies, waits for them, and re-layouts: 1.94 us -> none
    pallas_call x1, local copies, waits for them, and re-layouts: 0.68 us -> 1.45 us  [local(): pl.pallas_call(functools.partial(kernel, n_chan, n_seg), out_shape=jax.Sh...]
where the time goes in v3:
time: 52.3 us; the launch traced here: 52.2 us
  Pallas kernels  50.7 us (97%)
  local copies, waits for them, and re-layouts  1.45 us (3%)
    pallas_call x1, Pallas kernels, local(): pl.pallas_call(functools.partial(kernel, n_chan, n_seg), out_shape=jax.Sh...  50.7 us
    pallas_call x1, local copies, waits for them, and re-layouts, local(): pl.pallas_call(functools.partial(kernel, n_chan, n_seg), out_shape=jax.Sh...  1.45 us

profile of v3, /device:TPU:0, one launch (start us, length us, event | category | flops | bytes accessed | tf_op | source)
XLA Modules:
  0.0 52.2 jit_solution(669878745790550671)
XLA Ops:
  0.0 50.7 %shard_map.28 = f32[65,32]{1,0:T(8,128)} custom-call(bf16[128,2048]{1,0:T(8,128)(2,1)} %x_ref.1, s32[2,128,128]{2,1,0:T(8,128)} %b_ref.1), custom_call_target="tpu_custom_call" | custom-call | tf_op jit(solution)/shard_map/pallas_call | solution.py:443
  50.7 1.4 %copy.3 = f32[65,32]{0,1:T(8,128)} copy(f32[65,32]{1,0:T(8,128)} %shard_map.28) | data formatting | bytes 16640 | tf_op jit(solution)/shard_map/pallas_call | solution.py:443

commit v4 on v3

--- a/solution.py
+++ b/solution.py
@@ -19,7 +19,7 @@
 LANES = 128
 ROWS = 80
 TILE = 16
-GROUP = 8
+GROUP = 16
 MESH = pl.DeviceIdType.MESH
 CONTRACT = (((1,), (1,)), ((), ()))
 F32, BF16 = jnp.float32, jnp.bfloat16
@@ -87,7 +87,7 @@
     rows, length = source.shape
     count = length // LANES
 
-    @pl.loop(0, rows // TILE, unroll=True)
+    @pl.loop(0, rows // TILE)
     def _(g):
         here = pl.ds(pl.multiple_of(g * TILE, TILE), TILE)
         wide[here, NEAR * LANES : NEAR * LANES + length] = source[here, :]
@@ -99,7 +99,7 @@
 
 
 def spread_centre(block, start, rows, count):
-    @pl.loop(0, rows // TILE, unroll=True)
+    @pl.loop(0, rows // TILE)
     def _(g):
         here = pl.ds(pl.multiple_of(start + g * TILE, TILE), TILE)
 
@@ -126,30 +126,32 @@
         raw[pair * piece + k, : steps * rows, :] = out[:, k * width : (k + 1) * width]
 
 
-def bin_rows(raw, rows, group, factor, targets):
-    width = factor.shape[1]
-    scores = []
-    for x in range(group * GROUP, (group + 1) * GROUP):
-        each = jnp.broadcast_to(factor[x : x + 1, :], (FINE, width))
-        pieces = [raw[k, pl.ds(x, FINE, stride=rows), :] * each for k in range(COARSE)]
-        last = raw[COARSE - 1, pl.ds(FINE * rows + x, 1), :]
-        edge = jnp.broadcast_to(last, (FINE, width)) * each
-        scores.append(jnp.concatenate(pieces + [edge, edge], 0).astype(BF16))
-    score = jnp.concatenate(scores, 1)
+def bin_rows(raw, rows, start, factors, table, acc):
+    width = factors.shape[1]
     ids = lax.broadcasted_iota(jnp.int32, (NB, width), 0).astype(F32).astype(BF16)
     one, none = jnp.asarray(1, BF16), jnp.asarray(0, BF16)
-    for table, acc in targets:
-        hots = []
-        for x in range(group * GROUP, (group + 1) * GROUP):
-            hit = jnp.broadcast_to(table[x : x + 1, :].astype(BF16), (NB, width)) == ids
+
+    @pl.loop(0, rows // GROUP)
+    def _(g):
+        lead = pl.multiple_of(g * GROUP, GROUP)
+        here = pl.ds(pl.multiple_of(start + lead, GROUP), GROUP)
+        factor, bins = factors[here, :], table[here, :].astype(BF16)
+        last = raw[COARSE - 1, pl.ds(pl.multiple_of(FINE * rows + lead, GROUP), GROUP), :] * factor
+        scores, hots = [], []
+        for x in range(GROUP):
+            each = jnp.broadcast_to(factor[x : x + 1, :], (FINE, width))
+            pieces = [raw[k, pl.ds(lead + x, FINE, stride=rows), :] * each for k in range(COARSE)]
+            edge = jnp.broadcast_to(last[x : x + 1, :], (FINE, width))
+            scores.append(jnp.concatenate(pieces + [edge, edge], 0).astype(BF16))
+            hit = jnp.broadcast_to(bins[x : x + 1, :], (NB, width)) == ids
             hots.append(jnp.where(hit, one, none))
-        acc[...] += dot(jnp.concatenate(hots, 1), score)
+        acc[...] += dot(jnp.concatenate(hots, 1), jnp.concatenate(scores, 1))
 
 
 def kernel(
     n_chan, n_seg, x_ref, b_ref, o_ref,
-    trace, bins, cbuf, centres, nbuf, near_c, near_n, raw, i_sem, e_out, e_in, b_out, b_cross, b_near,
-    t_fwd, t_rev, t_two, f_one, f_two, acc_fwd, acc_rev, acc_two, squares, part, arrived, mine, others,
+    trace, bins, cbuf, centres, nbuf, near, raw, i_sem, e_out, e_in, b_out, b_cross, b_near,
+    tabs, factors, accs, squares, part, arrived, mine, others,
     e_send, e_recv, c_sem, x_send, x_recv, w_send, w_recv, n_send, n_recv, b_send, b_recv, r_send, r_recv, s_send, s_recv, known,
 ):
     channels, length = trace.shape
@@ -196,7 +198,7 @@
     trace_in.wait()
     squares[...] = jnp.zeros_like(squares)
 
-    @pl.loop(0, channels // TILE, unroll=True)
+    @pl.loop(0, channels // TILE)
     def _(g):
         here = pl.ds(pl.multiple_of(g * TILE, TILE), TILE)
         cols = [trace[here, at(i)].astype(F32) for i in range(count)]
@@ -210,9 +212,7 @@
     own_energy = jnp.sum(squares[...].T, axis=0, keepdims=True)
     e_out[...] = own_energy
     e_in[0, seg] = own_energy
-    acc_fwd[...] = jnp.zeros_like(acc_fwd)
-    acc_rev[...] = jnp.zeros_like(acc_rev)
-    acc_two[...] = jnp.zeros_like(acc_two)
+    accs[...] = jnp.zeros_like(accs)
     pl.semaphore_wait(barrier, len(peers))
 
     def tell(i):
@@ -265,7 +265,7 @@
         def _():
             to_below.start()
 
-        spread_near(own, near_c)
+        spread_near(own, near.at[0])
 
     @pl.when(helper)
     def _():
@@ -278,20 +278,11 @@
             to_wrap.start()
 
         to_twin.wait_recv()
-        spread_near(cbuf, near_c)
+        spread_near(cbuf, near.at[0])
 
     def forward(i, start):
         rows = cross_rows(start + i * size)
         return send(xbuf.at[rows], xbuf.at[rows], w_send.at[i], w_recv.at[i], (chan, twin))
-
-    pieces = size // GROUP
-
-    def advance(i, centre, near, after):
-        for p in range(pieces):
-            if centre is not None:
-                correlate(centre, near, raw.at[i % 2], p)
-            if after is not None:
-                bin_rows(raw.at[(i + 1) % 2], size, p, *after)
 
     def tables():
         for k in range(1, n_seg):
@@ -310,68 +301,87 @@
         own_scale, cross_scale, next_scale = scale(0), scale(1), scale(2)
         time_scale = 1.0 / math.sqrt(total_time)
         cross_column = jnp.broadcast_to(cross_scale, (channels, channels)).T
-        f_one[...] = cross_column * own_scale * time_scale
+        factors[0] = cross_column * own_scale * time_scale
         centre_scale = jnp.where(wrap, own_scale, cross_scale)
-        f_two[...] = jnp.broadcast_to(centre_scale, (channels, channels)).T * next_scale * time_scale
+        factors[1] = jnp.broadcast_to(centre_scale, (channels, channels)).T * next_scale * time_scale
         for copy in (bins_zero, bins_one):
             copy.wait_recv()
-        t_fwd[...] = bins[0].astype(F32).T
-        t_rev[...] = b_cross[...].astype(F32)
+        tabs[0] = bins[0].astype(F32).T
+        tabs[2, pl.ds(base, half), :] = b_cross[...].astype(F32)
 
         @pl.when(helper)
         def _():
-            t_two[...] = b_near[...].astype(F32).T
+            tabs[1] = b_near[...].astype(F32).T
 
         @pl.when(holder & (q != 0))
         def _():
-            t_two[...] = b_near[...].astype(F32)
+            tabs[1] = b_near[...].astype(F32)
 
         @pl.when(holder & (q == 0))
         def _():
-            t_two[...] = bins[1].astype(F32)
-
-    after = None
-    for i in range(2):
-        rows = cross_rows(base + i * size)
-        cross(i, 1).wait_recv()
-        forward(i, base).start()
-        spread_centre(centres.at[0], base + i * size, size, count)
-        advance(i, centres.at[0, rows], near_c, after)
-        if i == 0:
-            tables()
-        late = pl.ds(i * size, size)
-        after = (f_one.at[rows], ((t_fwd.at[rows], acc_fwd), (t_rev.at[late], acc_rev)))
+            tabs[1] = bins[1].astype(F32)
 
     @pl.when(wrap)
     def _():
         spread_centre(centres.at[1], 0, channels, count)
 
-    chosen = jnp.where(wrap, 1, 0)
-    to_above.wait_recv()
-    spread_near(nbuf, near_n)
-    for i in range(4):
-        if i < rounds:
-            pl.semaphore_wait(known.at[i], len(beside_us))
-            if i + 1 < rounds:
-                tell(i + 1)
-        start = (base if i < 2 else other_base) + (i % 2) * size
-        rows = cross_rows(start)
-        if i >= 2:
-            forward(i - 2, base).wait_recv()
+    def known_by(i):
+        pl.semaphore_wait(known.at[i], len(beside_us))
+
+        @pl.when(i + 1 < rounds)
+        def _():
+            tell(i + 1)
+
+    @pl.loop(0, 6)
+    def _(j):
+        phase = jnp.where(j >= 2, 1, 0)
+        start = jnp.where(j >= 4, other_base + (j - 4) * size, base + lax.rem(j, 2) * size)
+        start = pl.multiple_of(start, size)
+
+        @pl.when(j < 2)
+        def _():
+            cross(j, 1).wait_recv()
+            forward(j, base).start()
+
+        @pl.when(j >= 4)
+        def _():
+            forward(j - 4, base).wait_recv()
+
+        @pl.when((j < 2) | (j >= 4))
+        def _():
             spread_centre(centres.at[0], start, size, count)
-        advance(i, centres.at[chosen, rows], near_n, after)
-        after = (f_two.at[rows], ((t_two.at[rows], acc_two),))
+
+        @pl.when(j == 2)
+        def _():
+            to_above.wait_recv()
+            spread_near(nbuf, near.at[1])
+
+        @pl.when((j >= 2) & (j < 2 + rounds))
+        def _():
+            known_by(j - 2)
+
+        chosen = jnp.where(wrap, phase, 0)
+        for p in range(COARSE // 2):
+            correlate(centres.at[chosen, pl.ds(start, size)], near.at[phase], raw, p)
+
+        @pl.when(j == 0)
+        def _():
+            tables()
+
+        bin_rows(raw, size, start, factors.at[phase], tabs.at[phase], accs.at[phase])
+
+        @pl.when(j < 2)
+        def _():
+            bin_rows(raw, size, start, factors.at[0], tabs.at[2], accs.at[2])
+
     for i in range(4, rounds):
-        pl.semaphore_wait(known.at[i], len(beside_us))
-        if i + 1 < rounds:
-            tell(i + 1)
-    advance(4, None, None, after)
+        known_by(i)
 
     flip = lax.broadcasted_iota(jnp.int32, (ROWS, ROWS), 0) + lax.broadcasted_iota(jnp.int32, (ROWS, ROWS), 1)
     flip = jnp.where(flip == 2 * MAX_LAG, 1.0, 0.0).astype(F32)
-    two = acc_two[...]
-    ahead = acc_fwd[...] + jnp.where(holder, 0.0, two)
-    back = acc_rev[...] + jnp.where(holder, two, 0.0)
+    two = accs[1]
+    ahead = accs[0] + jnp.where(holder, 0.0, two)
+    back = accs[2] + jnp.where(holder, two, 0.0)
     turned = lax.dot_general(
         back, flip, (((1,), (0,)), ((), ())), precision=lax.Precision.HIGHEST, preferred_element_type=F32
     )
@@ -437,9 +447,6 @@
     owned = NB // n_chan
     dma = pltpu.SemaphoreType.DMA
     block = pltpu.VMEM((channels, length), BF16)
-    square = pltpu.VMEM((channels, channels), F32)
-    wide = pltpu.VMEM((channels, length + 2 * NEAR * LANES), BF16)
-    stacked = pltpu.VMEM((NB, ROWS), F32)
     return pl.pallas_call(
         functools.partial(kernel, n_chan, n_seg),
         out_shape=jax.ShapeDtypeStruct((LAGS, owned), F32),
@@ -450,16 +457,18 @@
             pltpu.VMEM((2, channels, channels), jnp.int32),
             block,
             pltpu.VMEM((2, channels, length + 2 * SPAN * LANES), BF16),
-            block, wide, wide,
-            pltpu.VMEM((2, COARSE, (FINE + 1) * size, channels), F32),
+            block,
+            pltpu.VMEM((2, channels, length + 2 * NEAR * LANES), BF16),
+            pltpu.VMEM((COARSE, (FINE + 1) * size, channels), F32),
             dma((2,)),
             pltpu.VMEM((1, channels), F32),
             pltpu.VMEM((3, n_seg, 1, channels), F32),
             pltpu.VMEM((2, channels, channels), BF16),
             pltpu.VMEM((channels // 2, channels), BF16),
             pltpu.VMEM((channels, channels), BF16),
-            square, pltpu.VMEM((channels // 2, channels), F32), square, square, square,
-            stacked, stacked, stacked,
+            pltpu.VMEM((3, channels, channels), F32),
+            pltpu.VMEM((2, channels, channels), F32),
+            pltpu.VMEM((3, NB, ROWS), F32),
             pltpu.VMEM((channels, LANES), F32),
             pltpu.VMEM((NB, LANES), F32),
             pltpu.VMEM((n_chan - 1, owned, LANES), F32),

time: 52.3 us -> 49.3 us (0.943)
  Pallas kernels: 50.7 us -> 47.6 us
    pallas_call x1, Pallas kernels: 50.7 us -> 47.6 us  [local(): pl.pallas_call(functools.partial(kernel, n_chan, n_seg), out_shape=jax.Sh...]
where the time goes in v4:
time: 49.3 us; the launch traced here: 49.1 us
  Pallas kernels  47.6 us (97%)
  local copies, waits for them, and re-layouts  1.45 us (3%)
    pallas_call x1, Pallas kernels, local(): pl.pallas_call(functools.partial(kernel, n_chan, n_seg), out_shape=jax.Sh...  47.6 us
    pallas_call x1, local copies, waits for them, and re-layouts, local(): pl.pallas_call(functools.partial(kernel, n_chan, n_seg), out_shape=jax.Sh...  1.45 us

profile of v4, /device:TPU:0, one launch (start us, length us, event | category | flops | bytes accessed | tf_op | source)
XLA Modules:
  0.0 49.1 jit_solution(4379489316004547016)
XLA Ops:
  0.0 47.6 %shard_map.28 = f32[65,32]{1,0:T(8,128)} custom-call(bf16[128,2048]{1,0:T(8,128)(2,1)} %x_ref.1, s32[2,128,128]{2,1,0:T(8,128)} %b_ref.1), custom_call_target="tpu_custom_call" | custom-call | tf_op jit(solution)/shard_map/pallas_call | solution.py:450
  47.6 1.4 %copy.3 = f32[65,32]{0,1:T(8,128)} copy(f32[65,32]{1,0:T(8,128)} %shard_map.28) | data formatting | bytes 16640 | tf_op jit(solution)/shard_map/pallas_call | solution.py:450
